TPU v7x, 256 devices: a whole 4x4x8 slice. The times are simulated.
256 devices in a mesh: role: 2 (over core), dev: 64 (over x_hi, y, z), head: 2 (over x_lo).
Axes of the slice: x: 4 (x_hi: 2, x_lo: 2; x = x_hi * 2 + x_lo), y: 4, z: 8, core: 2. Of those that a mesh axis runs over, the one named last changes fastest.
Arguments:
- hidden: bfloat16 [2048, 4096], P(('role', 'dev', 'head')), may hold values from -6 to 6
- queries: bfloat16 [2048, 64, 128], P(('role', 'dev'), 'head'), as said below
- cache_keys: bfloat16 [2048, 128, 4, 128], P(('role', 'dev'), None, 'head'), as said below
- cache_values: bfloat16 [2048, 128, 4, 128], P(('role', 'dev'), None, 'head'), may hold values from -6 to 6
- new_keys: bfloat16 [2048, 4, 128], P(('role', 'dev'), 'head'), may hold values from -6 to 6
- new_values: bfloat16 [2048, 4, 128], P(('role', 'dev'), 'head'), may hold values from -6 to 6
- lengths: int32 [2048], P(('role', 'dev')), may hold values from 32 to 128, as said below
- out_proj: bfloat16 [8192, 4096], P('head', 'dev'), may hold values from -0.5 to 0.5
- norm_gain: float32 [4096], replicated, may hold values from 0.1 to 1.9
- expert_gate: bfloat16 [128, 4096, 768], P(('role', 'dev'), None, 'head'), may hold values from -0.09375 to 0.09375
- expert_up: bfloat16 [128, 4096, 768], P(('role', 'dev'), None, 'head'), may hold values from -0.09375 to 0.09375
- expert_down: bfloat16 [128, 768, 4096], P(('role', 'dev'), 'head'), may hold values from -0.21875 to 0.21875
- expert_ids: int32 [2048, 8], P(('role', 'dev', 'head')), may hold values from 0 to 127, all different within a row; in each aligned block of 8 rows (0 to 7, 8 to 15, ...) at most 2 rows name the same one
- gate_levels: int32 [2048, 8], P(('role', 'dev', 'head')), may hold values from 1 to 255
Outputs:
- layer_out: bfloat16 [2048, 4096], P(('role', 'dev', 'head'))
Inputs may be any that keep to these rules, and one draw needn't show every extreme that they name: `queries`: query vectors of the new tokens. `cache_keys`: cached keys of the requests. `lengths`: the first request of each block of 16 rows holds 128 positions and the second holds 32. `expert_ids`: each row names 8 different experts; among the 8 rows of one device no expert is named more than 2 times, a bound that some block reaches.
All inputs are finite; a program needn't handle non-finite values.
Results may differ from a plain program's by a relative error of at most 0.0065.
Values may be sent and summed in bfloat16 or wider, within the bound.
No kernel may reach another device: no remote copies, remote signals or barrier semaphores. Data moves between devices by JAX's collectives and lax.ppermute only.
A program may use at most 64 MiB of HBM per device.

v0:
```python
import math
import jax
import jax.numpy as jnp
from jax import lax
from jax.sharding import PartitionSpec as P


def attend_block(query_rows, key_rows, value_rows, key_new, value_new, valid_len):
    row_count = query_rows.shape[0]
    kv_heads = key_rows.shape[2]
    group_size = query_rows.shape[1] // kv_heads
    head_dim = query_rows.shape[2]
    scaling = 1.0 / math.sqrt(head_dim)
    query_f = query_rows.astype(jnp.float32).reshape(row_count, kv_heads, group_size, head_dim)
    scores = jnp.einsum("bhgd,bthd->bhgt", query_f, key_rows.astype(jnp.float32)) * scaling
    scores_new = jnp.einsum("bhgd,bhd->bhg", query_f, key_new.astype(jnp.float32)) * scaling
    positions = jnp.arange(key_rows.shape[1], dtype=jnp.int32)
    usable = (positions[None, :] < valid_len[:, None])[:, None, None, :]
    masked = jnp.where(usable, scores, -1e30)
    highest = jnp.maximum(jnp.max(masked, axis=-1), scores_new)
    exp_terms = jnp.exp(masked - highest[..., None])
    exp_new = jnp.exp(scores_new - highest)
    totals = jnp.sum(exp_terms, axis=-1) + exp_new
    weights = (exp_terms / totals[..., None]).astype(jnp.bfloat16)
    weight_new = (exp_new / totals).astype(jnp.bfloat16)
    blended = jnp.einsum("bhgt,bthd->bhgd", weights, value_rows, preferred_element_type=jnp.float32)
    blended = (
        blended
        + weight_new.astype(jnp.float32)[..., None] * value_new.astype(jnp.float32)[:, :, None, :]
    )
    return blended.astype(jnp.bfloat16).reshape(row_count, kv_heads * group_size * head_dim)


def expert_rows(rows_in, gate_w, up_w, down_w):
    gate_part = jnp.dot(rows_in, gate_w, preferred_element_type=jnp.float32)
    up_part = jnp.dot(rows_in, up_w, preferred_element_type=jnp.float32)
    active = (jax.nn.silu(gate_part) * up_part).astype(jnp.bfloat16)
    return jnp.dot(active, down_w, preferred_element_type=jnp.float32)


def slot_ranks(flat_ids, experts):
    one_hot = (flat_ids[:, None] == jnp.arange(experts, dtype=jnp.int32)[None, :]).astype(jnp.int32)
    return jnp.sum(jnp.cumsum(one_hot, axis=0) * one_hot, axis=1) - 1


def on_device(
    hidden,
    queries,
    cache_keys,
    cache_values,
    new_keys,
    new_values,
    lengths,
    out_proj,
    norm_gain,
    expert_gate,
    expert_up,
    expert_down,
    expert_ids,
    gate_levels,
):
    attended = attend_block(queries, cache_keys, cache_values, new_keys, new_values, lengths)
    columns = jnp.dot(
        lax.all_gather(attended, "dev", axis=0, tiled=True),
        out_proj,
        preferred_element_type=jnp.float32,
    )
    dev_count = lax.axis_size("dev")
    head_count = lax.axis_size("head")
    experts = lax.axis_size("role") * dev_count
    col_width = out_proj.shape[1]
    width = dev_count * col_width
    projected = lax.all_to_all(columns, ("dev", "head"), split_axis=0, concat_axis=1, tiled=True)
    tokens = projected.shape[0]
    summed = jnp.sum(projected.reshape(tokens, dev_count, head_count, col_width), axis=2).reshape(
        tokens, width
    )
    residual = hidden.astype(jnp.float32) + summed
    normed = (
        residual
        * lax.rsqrt(jnp.mean(residual * residual, axis=-1, keepdims=True) + 1e-06)
        * norm_gain
    ).astype(jnp.bfloat16)
    top_k = expert_ids.shape[1]
    capacity = max(2, 2 * tokens * top_k // experts)
    own_ids = expert_ids.reshape(-1)
    own_ranks = slot_ranks(own_ids, experts)
    pair_rows, pair_ids = (
        lax.all_gather(normed, "head", axis=0, tiled=True),
        lax.all_gather(expert_ids, "head", axis=0, tiled=True),
    )
    pair_flat = pair_ids.reshape(head_count, tokens * top_k)
    pair_ranks = jax.vmap(lambda id_row: slot_ranks(id_row, experts))(pair_flat)
    pair_ranks = pair_ranks + capacity * jnp.arange(head_count, dtype=jnp.int32)[:, None]
    rows_from = jnp.arange(head_count * tokens * top_k, dtype=jnp.int32) // top_k
    outgoing = (
        jnp.zeros((experts, head_count * capacity, width), jnp.bfloat16)
        .at[pair_flat.reshape(-1), pair_ranks.reshape(-1)]
        .set(pair_rows[rows_from])
    )
    incoming = lax.all_to_all(outgoing, ("role", "dev"), split_axis=0, concat_axis=0, tiled=True)
    sources = incoming.shape[0]
    slot_total = incoming.shape[1]
    partial_value = expert_rows(
        incoming.reshape(sources * slot_total, width), expert_gate[0], expert_up[0], expert_down[0]
    )
    partial_value = partial_value.reshape(sources, slot_total, width).astype(jnp.bfloat16)
    arrived = lax.all_to_all(
        partial_value, ("role", "dev"), split_axis=0, concat_axis=0, tiled=True
    )
    arrived = (
        lax.psum_scatter(arrived, "head", scatter_dimension=1, tiled=True)
        .astype(jnp.float32)
        .astype(jnp.bfloat16)
    )
    picked = arrived[own_ids, own_ranks].astype(jnp.float32).reshape(tokens, top_k, width)
    levels = gate_levels.astype(jnp.float32)
    shares = levels / jnp.sum(levels, axis=1, keepdims=True)
    return (residual + jnp.sum(shares[..., None] * picked, axis=1)).astype(jnp.bfloat16)


def solution(mesh):
    placed = (
        P(("role", "dev", "head"), None),
        P(("role", "dev"), "head", None),
        P(("role", "dev"), None, "head", None),
        P(("role", "dev"), None, "head", None),
        P(("role", "dev"), "head", None),
        P(("role", "dev"), "head", None),
        P(("role", "dev")),
        P("head", "dev"),
        P(),
        P(("role", "dev"), None, "head"),
        P(("role", "dev"), None, "head"),
        P(("role", "dev"), "head", None),
        P(("role", "dev", "head"), None),
        P(("role", "dev", "head"), None),
    )
    return jax.shard_map(
        on_device,
        mesh=mesh,
        in_specs=placed,
        out_specs=P(("role", "dev", "head"), None),
        check_vma=False,
    )
```

profile of v0, /device:TPU:1, one launch (start us, length us, event | category | flops | bytes accessed | tf_op | source)
XLA Modules:
  0.0 560.9 jit_solution(16563779175409254275)
XLA Ops:
  6.5 0.0 copy-start
  6.5 0.0 all-gather.2.cloned.1.call-start
  6.5 0.9 iota_compare_fusion.2
  7.4 1.1 fusion.22
  8.6 2.1 fusion.34
  10.7 0.3 fusion.17
  11.0 0.7 convert_element_type.55
  11.7 1.7 fusion.12
  13.4 0.7 copy.53
  14.1 0.0 all-gather.2.cloned.1.call-update
  14.1 0.0 copy-done.4
  14.1 3.7 all_gather.10
  17.9 0.1 eq.30
  18.0 0.1 fusion.20
  18.1 0.1 reduce_window_sum.22
  18.2 0.2 select_reduce_fusion
  18.3 148.0 %all-gather.2.cloned.1.call-done = bf16[1024,4096]{1,0:T(8,128)(2,1)} async-done(((bf16[16,4096]{1,0:T(8,128)(2,1)}), bf16[1024,4096]{1,0:T(8,128)(2,1)}) %all-gather.2.cloned.1.call-update) | async-done | bytes 8388624 | tf_op jit(solution)/shard_map/all_gather | solution.py:64
  166.3 6.6 %convolution_bitcast_fusion = f32[128,8,64]{2,1,0:T(8,128)} fusion(bf16[1024,4096]{1,0:T(8,128)(2,1)} %all-gather.2.cloned.1.call-done, bf16[4096,64]{0,1:T(8,128)(2,1)} %param.21), kind=kOutput, calls=%fused_computation.11 | convolution fusion | flops 536870912 | bytes 9175040 | tf_op jit(solution)/shard_map/dot_general | solution.py:63
  172.9 2.1 reshape.251
  175.0 9.4 %all-to-all-start = ((f32[128,1,512]{2,1,0:T(1,128)}), f32[128,1,512]{2,1,0:T(1,128)S(1)}, u32[]{:S(2)}, u32[]{:S(2)}) async-start(f32[128,1,512]{2,1,0:T(1,128)} %reshape.251), calls=%async_computation | async-start | bytes 524288 | tf_op jit(solution)/shard_map/all_to_all | solution.py:73
  184.5 0.0 reduce-scatter.2.cloned.1.call-start
  184.5 0.1 add_add_fusion
  184.6 0.1 reshape_reshape.3
  184.7 0.1 add.149
  184.8 11.2 %all-to-all-done = f32[128,1,512]{2,1,0:T(1,128)S(1)} async-done(((f32[128,1,512]{2,1,0:T(1,128)}), f32[128,1,512]{2,1,0:T(1,128)S(1)}, u32[]{:S(2)}, u32[]{:S(2)}) %all-to-all-start) | async-done | bytes 262176 | tf_op jit(solution)/shard_map/all_to_all | solution.py:73
  196.0 0.7 copy-done.2
  196.7 0.5 broadcast.263
  197.2 2.2 reduce
  199.5 0.9 reshape.252
  200.4 1.1 bitcast_reduce_fusion
  201.5 0.7 copy.33
  202.3 1.1 reshape.224
  203.3 0.0 copy-done.3
  203.3 0.1 multiply_reduce_fusion
  203.5 0.1 multiply_convert_fusion
  203.6 3.8 all_gather.11
  207.4 2.2 gather_fusion
  209.5 4.0 broadcast_in_dim.16
  213.6 32.4 %scatter_fusion = bf16[128,4,4096]{2,1,0:T(4,128)(2,1)} fusion(bf16[128,4,4096]{2,1,0:T(4,128)(2,1)} %broadcast_in_dim.16, s32[128]{0:T(128)S(1)} %fusion.32, bf16[128,4096]{1,0:T(8,128)(2,1)} %gather_fusion), kind=kCustom, calls=%fused_computation.2 | custom fusion | bytes 3146752 | tf_op jit(solution)/shard_map/scatter | solution.py:99
  246.0 112.3 %all_to_all.26 = bf16[128,4,4096]{2,1,0:T(4,128)(2,1)} all-to-all(bf16[128,4,4096]{2,1,0:T(4,128)(2,1)} %scatter_fusion), channel_id=1, replica_groups=mesh['role'=2,'dev'=64,'head'=2] {'role','dev'}, dimensions={0} | all-to-all | bytes 8388608 | tf_op jit(solution)/shard_map/all_to_all | solution.py:101
  358.3 6.9 %reshape.225 = bf16[512,4096]{1,0:T(8,128)(2,1)} reshape(bf16[128,4,4096]{2,1,0:T(4,128)(2,1)} %all_to_all.26) | data formatting | bytes 8388608 | tf_op jit(solution)/shard_map/reshape | solution.py:105
  365.2 5.6 %fusion.3 = f32[512,384]{1,0:T(8,128)S(1)} fusion(bf16[512,4096]{1,0:T(8,128)(2,1)} %reshape.225, bf16[1,4096,384]{2,1,0:T(8,128)(2,1)} %param.23), kind=kOutput, calls=%fused_computation.7 | convolution fusion | flops 1610612736 | bytes 8126464 | tf_op jit(solution)/shard_map/dot_general | solution.py:35
  370.8 0.0 copy-done.1
  370.8 0.0 copy-done.7
  370.8 3.1 fusion.8
  373.9 1.8 dot_general.29
  375.8 3.3 convolution_convert_fusion
  379.1 3.2 copy.35
  382.3 104.9 %all_to_all.27 = bf16[128,4,4096]{2,1,0:T(4,128)(2,1)S(1)} all-to-all(bf16[128,4,4096]{2,1,0:T(4,128)(2,1)S(1)} %copy.35), channel_id=1, replica_groups=mesh['role'=2,'dev'=64,'head'=2] {'role','dev'}, dimensions={0} | all-to-all | bytes 8388608 | tf_op jit(solution)/shard_map/all_to_all | solution.py:108
  487.3 4.2 copy.36
  491.5 0.0 reduce-scatter.2.cloned.1.call-update
  491.5 0.1 eq.34
  491.6 0.1 reshape.226
  491.7 0.1 fusion.21
  491.7 0.1 reduce_window_sum.23
  491.8 0.3 copy-done.6
  492.2 0.1 convert_reduce_fusion
  492.3 0.2 select_reduce_fusion.1
  492.5 0.1 convert_divide_fusion
  492.6 50.9 %reduce-scatter.2.cloned.1.call-done = bf16[128,2,4096]{2,0,1:T(8,128)(2,1)} async-done(((bf16[128,4,4096]{2,0,1:T(8,128)(2,1)}), bf16[128,2,4096]{2,0,1:T(8,128)(2,1)}) %reduce-scatter.2.cloned.1.call-update) | async-done | bytes 2097168 | tf_op jit(solution)/shard_map/reduce_scatter | solution.py:112
  543.5 5.1 copy.37
  548.6 3.3 gather_fusion.1
  551.9 1.5 fusion.13
  553.4 0.7 add_convert_fusion
  (17 shorter events, 0.1 us)
Async XLA Ops:
  6.5 369.2 %copy-start = (bf16[1,384,4096]{2,1,0:T(8,128)(2,1)S(1)}, bf16[1,384,4096]{2,1,0:T(8,128)(2,1)}, u32[]{:S(2)}) copy-start(bf16[1,384,4096]{2,1,0:T(8,128)(2,1)} %param.25) | copy-start | bytes 9437188
  6.5 7.6 %copy-start.4 = (s32[8,8]{1,0:T(8,128)S(1)}, s32[8,8]{1,0:T(8,128)}, u32[]{:S(2)}) copy-start(s32[8,8]{1,0:T(8,128)} %param.26) | copy-start | bytes 772
  6.5 159.8 %all-gather.2.cloned.1.call-start = ((), (), s32[]{:S(2)}) async-start(), calls=%async_computation.4 | async-start | bytes 8519680 | tf_op jit(solution)/shard_map/all_gather | solution.py:64
  172.9 30.4 %copy-start.3 = (bf16[8,4096]{1,0:T(8,128)(2,1)S(1)}, bf16[8,4096]{1,0:T(8,128)(2,1)}, u32[]{:S(2)}) copy-start(bf16[8,4096]{1,0:T(8,128)(2,1)} %param.14) | copy-start | bytes 196612
  172.9 30.6 %copy-start.5 = (f32[4096]{0:T(1024)S(1)}, f32[4096]{0:T(1024)}, u32[]{:S(2)}) copy-start(f32[4096]{0:T(1024)} %param.22) | copy-start | bytes 49156
  175.0 21.0 %all-to-all-start = ((f32[128,1,512]{2,1,0:T(1,128)}), f32[128,1,512]{2,1,0:T(1,128)S(1)}, u32[]{:S(2)}, u32[]{:S(2)}) async-start(f32[128,1,512]{2,1,0:T(1,128)} %reshape.251), calls=%async_computation | async-start | bytes 524288 | tf_op jit(solution)/shard_map/all_to_all | solution.py:73
  184.5 359.0 %reduce-scatter.2.cloned.1.call-start = ((), (), s32[]{:S(2)}) async-start(), calls=%async_computation.5 | async-start | bytes 6291456 | tf_op jit(solution)/shard_map/reduce_scatter | solution.py:112
  196.0 0.7 copy-start.2
  365.2 5.6 %copy-start.1 = (bf16[512,4096]{1,0:T(8,128)(2,1)S(1)}, bf16[512,4096]{1,0:T(8,128)(2,1)}, u32[]{:S(2)}) copy-start(bf16[512,4096]{1,0:T(8,128)(2,1)} %reshape.225) | copy-start | bytes 12582916
  365.2 5.6 %copy-start.7 = (bf16[1,4096,384]{2,1,0:T(8,128)(2,1)S(1)}, bf16[1,4096,384]{2,1,0:T(8,128)(2,1)}, u32[]{:S(2)}) copy-start(bf16[1,4096,384]{2,1,0:T(8,128)(2,1)} %param.24) | copy-start | bytes 9437188
  491.5 0.7 copy-start.6
Sparse Core Ops, SparseCore 0:
  14.3 152.0 all-gather.1
  491.6 51.7 reduce-scatter.1
where the time goes:
time: 562 us; the launch traced here: 561 us
  blocking collectives  225 us (40%)
  waiting for transfers between devices  210 us (37%)
  local copies, waits for them, and re-layouts  70.8 us (13%)
  matrix products  23.5 us (4%)
  between operations  13.6 us (2%)
  starting transfers between devices  9.48 us (2%)
  other arithmetic  8.69 us (2%)
    all_gather x1, waiting for transfers between devices, on_device(): lax.all_gather(attended, 'dev', axis=0, tiled=True)  148 us
    all_to_all x1, blocking collectives, on_device(): lax.all_to_all(outgoing, ('role', 'dev'), split_axis=0, concat_axis=0, ti...  112 us
    all_to_all x1, blocking collectives, on_device(): lax.all_to_all(partial_value, ('role', 'dev'), split_axis=0, concat_axis=...  105 us
    reduce_scatter x1, waiting for transfers between devices, on_device(): lax.psum_scatter(arrived, 'head', scatter_dimension=1, tiled=True)  50.9 us
    scatter x1, local copies, waits for them, and re-layouts, on_device(): outgoing = jnp.zeros((experts, head_count * capacity, width), jnp.bfloat1...  32.4 us
  transfers between devices with their start and end apart: 3, of which 3 were waited for; matrix products, arithmetic and copies ran while one was open for 0% of the time, Pallas kernels for 0%

commit v1 on v0

--- a/solution.py
+++ b/solution.py
@@ -61,7 +61,9 @@
 ):
     attended = attend_block(queries, cache_keys, cache_values, new_keys, new_values, lengths)
     columns = jnp.dot(
-        lax.all_gather(attended, "dev", axis=0, tiled=True),
+        jnp.concatenate(
+            lax.all_to_all(jnp.stack([attended] * lax.axis_size("dev")), "dev", 0, 0), axis=0
+        ),
         out_proj,
         preferred_element_type=jnp.float32,
     )

time: 562 us -> 615 us (1.094)
  starting transfers between devices: 9.48 us -> 29.4 us
  blocking collectives: 225 us -> 241 us
  waiting for transfers between devices: 210 us -> 223 us
    all_to_all x0 -> x1, waiting for transfers between devices: none -> 161 us  [on_device(): lax.all_to_all(jnp.stack([attended] * lax.axis_size('dev')), 'dev', 0, 0)]
    all_gather x1 -> x0, waiting for transfers between devices: 148 us -> none  [on_device(): lax.all_gather(attended, 'dev', axis=0, tiled=True)]
    all_gather x1, blocking collectives: 3.74 us -> 21.4 us  [on_device(): lax.all_gather(expert_ids, 'head', axis=0, tiled=True)]
    all_to_all x0 -> x1, starting transfers between devices: none -> 15.5 us  [on_device(): lax.all_to_all(jnp.stack([attended] * lax.axis_size('dev')), 'dev', 0, 0)]
where the time goes in v1:
time: 615 us; the launch traced here: 614 us
  blocking collectives  241 us (39%)
  waiting for transfers between devices  223 us (36%)
  local copies, waits for them, and re-layouts  74.4 us (12%)
  starting transfers between devices  29.4 us (5%)
  matrix products  23.5 us (4%)
  between operations  13.6 us (2%)
  other arithmetic  8.69 us (1%)
    all_to_all x1, waiting for transfers between devices, on_device(): lax.all_to_all(jnp.stack([attended] * lax.axis_size('dev')), 'dev', 0, 0)  161 us
    all_to_all x1, blocking collectives, on_device(): lax.all_to_all(outgoing, ('role', 'dev'), split_axis=0, concat_axis=0, ti...  111 us
    all_to_all x1, blocking collectives, on_device(): lax.all_to_all(partial_value, ('role', 'dev'), split_axis=0, concat_axis=...  105 us
    reduce_scatter x1, waiting for transfers between devices, on_device(): lax.psum_scatter(arrived, 'head', scatter_dimension=1, tiled=True)  50.9 us
    scatter x1, local copies, waits for them, and re-layouts, on_device(): outgoing = jnp.zeros((experts, head_count * capacity, width), jnp.bfloat1...  32.4 us
    all_gather x1, blocking collectives, on_device(): lax.all_gather(expert_ids, 'head', axis=0, tiled=True)  21.4 us
    all_to_all x1, starting transfers between devices, on_device(): lax.all_to_all(jnp.stack([attended] * lax.axis_size('dev')), 'dev', 0, 0)  15.5 us
    all_to_all x1, starting transfers between devices, on_device(): lax.all_to_all(columns, ('dev', 'head'), split_axis=0, concat_axis=1, til...  13.9 us
  transfers between devices with their start and end apart: 3, of which 3 were waited for; matrix products, arithmetic and copies ran while one was open for 0% of the time, Pallas kernels for 0%

profile of v1, /device:TPU:1, one launch (start us, length us, event | category | flops | bytes accessed | tf_op | source)
XLA Modules:
  0.0 613.8 jit_solution(7271716496908145338)
XLA Ops:
  6.5 0.0 copy-start
  6.5 0.9 iota_compare_fusion.2
  7.4 1.1 fusion.24
  8.6 2.1 fusion.36
  10.7 0.3 fusion.19
  11.0 0.7 convert_element_type.55
  11.7 1.7 fusion.12
  13.4 0.1 copy.51
  13.4 4.3 stack.3
  17.7 15.5 %all-to-all-start = ((bf16[64,16,4096]{2,1,0:T(8,128)(2,1)}), bf16[64,16,4096]{2,1,0:T(8,128)(2,1)}, u32[]{:S(2)}, u32[]{:S(2)}) async-start(bf16[64,16,4096]{2,1,0:T(8,128)(2,1)} %stack.3), calls=%async_computation | async-start | bytes 16777216 | tf_op jit(solution)/shard_map/all_to_all | solution.py:65
  33.2 0.0 copy-done.5
  33.2 21.4 %all_gather.6 = s32[16,8]{1,0:T(8,128)S(1)} all-gather(s32[8,8]{1,0:T(8,128)S(1)} %copy-done.5), channel_id=1, replica_groups=mesh['role'=2,'dev'=64,'head'=2] {'head'}, dimensions={0}, use_global_device_ids=true | all-gather | bytes 768 | tf_op jit(solution)/shard_map/all_gather | solution.py:92
  54.6 0.1 eq.30
  54.7 0.1 fusion.22
  54.8 0.1 reduce_window_sum.22
  54.9 0.2 select_reduce_fusion
  55.1 160.8 %all-to-all-done = bf16[64,16,4096]{2,1,0:T(8,128)(2,1)} async-done(((bf16[64,16,4096]{2,1,0:T(8,128)(2,1)}), bf16[64,16,4096]{2,1,0:T(8,128)(2,1)}, u32[]{:S(2)}, u32[]{:S(2)}) %all-to-all-start) | async-done | bytes 8388640 | tf_op jit(solution)/shard_map/all_to_all | solution.py:65
  215.9 6.6 %fusion.16 = f32[128,8,64]{2,1,0:T(8,128)} fusion(bf16[128,8,4096]{2,1,0:T(8,128)(2,1)} %bitcast.4, bf16[4096,64]{0,1:T(8,128)(2,1)} %param.21), kind=kOutput, calls=%fused_computation.20 | convolution fusion | flops 536870912 | bytes 9175040 | tf_op jit(solution)/shard_map/dot_general | solution.py:63
  222.5 2.1 reshape.253
  224.6 13.9 %all-to-all-start.1 = ((f32[128,1,512]{2,1,0:T(1,128)}), f32[128,1,512]{2,1,0:T(1,128)S(1)}, u32[]{:S(2)}, u32[]{:S(2)}) async-start(f32[128,1,512]{2,1,0:T(1,128)} %reshape.253), calls=%async_computation.1 | async-start | bytes 524288 | tf_op jit(solution)/shard_map/all_to_all | solution.py:75
  238.5 0.0 reduce-scatter.2.cloned.1.call-start
  238.5 0.1 add_add_fusion
  238.6 0.1 reshape_reshape.3
  238.7 0.1 add.149
  238.8 11.3 %all-to-all-done.1 = f32[128,1,512]{2,1,0:T(1,128)S(1)} async-done(((f32[128,1,512]{2,1,0:T(1,128)}), f32[128,1,512]{2,1,0:T(1,128)S(1)}, u32[]{:S(2)}, u32[]{:S(2)}) %all-to-all-start.1) | async-done | bytes 262176 | tf_op jit(solution)/shard_map/all_to_all | solution.py:75
  250.1 0.7 copy-done.2
  250.8 0.5 broadcast.264
  251.3 2.2 reduce
  253.6 0.9 reshape.254
  254.5 1.1 bitcast_reduce_fusion
  255.6 0.7 copy.32
  256.4 1.1 reshape.225
  257.4 0.2 multiply_reduce_fusion
  257.6 0.1 multiply_convert_fusion
  257.7 4.0 all_gather.7
  261.7 2.2 gather_fusion
  263.8 4.0 broadcast_in_dim.16
  267.9 32.4 %scatter_fusion = bf16[128,4,4096]{2,1,0:T(4,128)(2,1)} fusion(bf16[128,4,4096]{2,1,0:T(4,128)(2,1)} %broadcast_in_dim.16, s32[128]{0:T(128)S(1)} %fusion.34, bf16[128,4096]{1,0:T(8,128)(2,1)} %gather_fusion), kind=kCustom, calls=%fused_computation.2 | custom fusion | bytes 3146752 | tf_op jit(solution)/shard_map/scatter | solution.py:101
  300.3 110.8 %all_to_all.28 = bf16[128,4,4096]{2,1,0:T(4,128)(2,1)} all-to-all(bf16[128,4,4096]{2,1,0:T(4,128)(2,1)} %scatter_fusion), channel_id=1, replica_groups=mesh['role'=2,'dev'=64,'head'=2] {'role','dev'}, dimensions={0} | all-to-all | bytes 8388608 | tf_op jit(solution)/shard_map/all_to_all | solution.py:103
  411.1 6.9 %reshape.226 = bf16[512,4096]{1,0:T(8,128)(2,1)} reshape(bf16[128,4,4096]{2,1,0:T(4,128)(2,1)} %all_to_all.28) | data formatting | bytes 8388608 | tf_op jit(solution)/shard_map/reshape | solution.py:107
  418.0 5.6 fusion.3
  423.7 0.0 copy-done.1
  423.7 0.0 copy-done.8
  423.7 3.1 fusion.8
  426.8 1.8 dot_general.32
  428.6 3.3 convolution_convert_fusion
  432.0 3.2 copy.34
  435.2 104.9 %all_to_all.29 = bf16[128,4,4096]{2,1,0:T(4,128)(2,1)S(1)} all-to-all(bf16[128,4,4096]{2,1,0:T(4,128)(2,1)S(1)} %copy.34), channel_id=1, replica_groups=mesh['role'=2,'dev'=64,'head'=2] {'role','dev'}, dimensions={0} | all-to-all | bytes 8388608 | tf_op jit(solution)/shard_map/all_to_all | solution.py:110
  540.1 4.2 copy.35
  544.4 0.0 reduce-scatter.2.cloned.1.call-update
  544.4 0.1 eq.34
  544.5 0.1 reshape.227
  544.5 0.1 fusion.23
  544.6 0.1 reduce_window_sum.23
  544.7 0.3 copy-done.7
  545.0 0.1 convert_reduce_fusion
  545.2 0.2 select_reduce_fusion.1
  545.3 0.1 convert_divide_fusion
  545.4 50.9 %reduce-scatter.2.cloned.1.call-done = bf16[128,2,4096]{2,0,1:T(8,128)(2,1)} async-done(((bf16[128,4,4096]{2,0,1:T(8,128)(2,1)}), bf16[128,2,4096]{2,0,1:T(8,128)(2,1)}) %reduce-scatter.2.cloned.1.call-update) | async-done | bytes 2097168 | tf_op jit(solution)/shard_map/reduce_scatter | solution.py:114
  596.3 5.1 copy.36
  601.5 3.3 gather_fusion.1
  604.8 1.5 fusion.13
  606.3 0.0 copy-done.4
  606.3 0.7 add_convert_fusion
  (19 shorter events, 0.1 us)
Async XLA Ops:
  6.5 422.1 %copy-start = (bf16[1,384,4096]{2,1,0:T(8,128)(2,1)S(1)}, bf16[1,384,4096]{2,1,0:T(8,128)(2,1)}, u32[]{:S(2)}) copy-start(bf16[1,384,4096]{2,1,0:T(8,128)(2,1)} %param.25) | copy-start | bytes 9437188
  17.7 15.5 %copy-start.5 = (s32[8,8]{1,0:T(8,128)S(1)}, s32[8,8]{1,0:T(8,128)}, u32[]{:S(2)}) copy-start(s32[8,8]{1,0:T(8,128)} %param.26) | copy-start | bytes 772
  17.7 198.2 %all-to-all-start = ((bf16[64,16,4096]{2,1,0:T(8,128)(2,1)}), bf16[64,16,4096]{2,1,0:T(8,128)(2,1)}, u32[]{:S(2)}, u32[]{:S(2)}) async-start(bf16[64,16,4096]{2,1,0:T(8,128)(2,1)} %stack.3), calls=%async_computation | async-start | bytes 16777216 | tf_op jit(solution)/shard_map/all_to_all | solution.py:65
  222.5 34.9 %copy-start.3 = (bf16[8,4096]{1,0:T(8,128)(2,1)S(1)}, bf16[8,4096]{1,0:T(8,128)(2,1)}, u32[]{:S(2)}) copy-start(bf16[8,4096]{1,0:T(8,128)(2,1)} %param.14) | copy-start | bytes 196612
  222.5 35.1 %copy-start.6 = (f32[4096]{0:T(1024)S(1)}, f32[4096]{0:T(1024)}, u32[]{:S(2)}) copy-start(f32[4096]{0:T(1024)} %param.22) | copy-start | bytes 49156
  224.6 25.5 %all-to-all-start.1 = ((f32[128,1,512]{2,1,0:T(1,128)}), f32[128,1,512]{2,1,0:T(1,128)S(1)}, u32[]{:S(2)}, u32[]{:S(2)}) async-start(f32[128,1,512]{2,1,0:T(1,128)} %reshape.253), calls=%async_computation.1 | async-start | bytes 524288 | tf_op jit(solution)/shard_map/all_to_all | solution.py:75
  238.5 357.8 %reduce-scatter.2.cloned.1.call-start = ((), (), s32[]{:S(2)}) async-start(), calls=%async_computation.5 | async-start | bytes 6291456 | tf_op jit(solution)/shard_map/reduce_scatter | solution.py:114
  250.1 0.7 copy-start.2
  418.0 5.6 copy-start.1
  418.0 5.6 copy-start.8
  544.4 0.7 copy-start.7
  545.4 60.9 %copy-start.4 = (bf16[8,4096]{1,0:T(8,128)(2,1)S(1)}, bf16[8,4096]{1,0:T(8,128)(2,1)}, u32[]{:S(2)}) copy-start(bf16[8,4096]{1,0:T(8,128)(2,1)} %param.14) | copy-start | bytes 196612
Sparse Core Ops, SparseCore 0:
  544.5 51.7 reduce-scatter.1
